TPU v7x, 32 devices: a whole 2x2x4 slice. The times are simulated.
32 devices in a mesh: frames: 4 (over y, core), win: 8 (over z, x).
Axes of the slice: x: 2, y: 2, z: 4, core: 2. Of those that a mesh axis runs over, the one named last changes fastest.
Arguments:
- memberships: float32 [8, 256, 4096], P('win', 'frames'), as said below
- lag_times: int32 [8], P('win'), may hold values from 1 to 8, as said below
- segment_ids: int32 [8, 256], P('win'), may hold values from 0 to 7, never falling along the last dimension, each value on 1 to 128 neighbouring positions
- bias_codes: int32 [8, 4096], P('win'), may hold values from 0 to 511
Outputs:
- free_energy: float32 [4096], P('frames')
- log_multipliers: float32 [8, 4096], P('win', 'frames')
Inputs may be any that keep to these rules, and one draw needn't show every extreme that they name: Positive; each frame's memberships sum to one up to rounding. `lag_times`: some window's lag time is 8.
All inputs are finite; a program needn't handle non-finite values.
Results may differ from a plain program's by a relative error of at most 0.00041.
Values may be sent and summed in bfloat16 or wider, within the bound.
No kernel may reach another device: no remote copies, remote signals or barrier semaphores. Data moves between devices by JAX's collectives and lax.ppermute only.
A program may use at most 64 MiB of HBM per device.

v0:
```python
import jax
import jax.numpy as jnp
from jax import lax
from jax.sharding import PartitionSpec as P

LAGMAX = 8
ITERS = 2
bias_unit = 1.0 / 128.0


def shifted(block, axis, distance):
    devices = range(lax.axis_size(axis))
    route = [(i - distance, i) for i in devices if i - distance in devices]
    return lax.ppermute(block, axis, route)


def split_rows(block, frames_dev, lag_time, valid_all):
    width = frames_dev + LAGMAX
    number = block.shape[0] // width
    states = block.shape[1]
    shaped = block.reshape(number, width, states)
    current = shaped[:, :frames_dev].reshape(number * frames_dev, states)
    later = lax.dynamic_slice_in_dim(shaped, lag_time, frames_dev, 1).reshape(
        number * frames_dev, states
    )
    later = jnp.where(valid_all[:, None], later, jnp.zeros((), later.dtype))
    return (current, later)


def add_pair(accumulated, current, later, first, rows):
    current_cols = lax.dynamic_slice_in_dim(current, first, rows, 1)
    later_cols = lax.dynamic_slice_in_dim(later, first, rows, 1)
    accumulated = jnp.einsum("tr,ts->rs", current_cols, later, preferred_element_type=jnp.float32)
    return accumulated + jnp.einsum(
        "tr,ts->rs", later_cols, current, preferred_element_type=jnp.float32
    )


def shards(memberships, lag_times, segment_ids, bias_codes):
    member = memberships[0].astype(jnp.bfloat16)
    lag_time = lag_times[0]
    segment_row = segment_ids[0]
    frames_dev = member.shape[0]
    states = member.shape[1]
    frames_all = segment_row.shape[0]
    rows = states // lax.axis_size("frames")
    position = lax.axis_index("frames")
    first = position * rows
    heading = shifted(member[:LAGMAX], "frames", -1)
    extended = jnp.concatenate([member, heading], axis=0)
    segment_ext = jnp.concatenate([segment_row, jnp.full((LAGMAX,), -1, jnp.int32)])
    valid_all = segment_row == lax.dynamic_slice_in_dim(segment_ext, lag_time, frames_all, 0)
    empty = jnp.zeros((rows, states), jnp.float32)
    current, later = split_rows(
        lax.all_gather(extended, "frames", axis=0, tiled=True), frames_dev, lag_time, valid_all
    )
    sym_counts = add_pair(empty, current, later, first, rows)
    gammas = jnp.exp(-bias_codes[0].astype(jnp.float32) * bias_unit)
    gamma_rows = lax.dynamic_slice_in_dim(gammas, first, rows, 0)
    mult_rows = jnp.sum(sym_counts, axis=1) * 0.5
    mult_full = lax.all_gather(mult_rows, "frames", axis=0, tiled=True)
    window_total = jnp.sum(mult_full)
    count_rows = lax.psum(mult_rows, "win")
    weights = jnp.full((states,), 1.0 / states, jnp.float32)
    for sweep in range(ITERS):
        scaled = gammas * weights
        scaled_rows = lax.dynamic_slice_in_dim(scaled, first, rows, 0)
        denom = mult_rows[:, None] * scaled[None, :] + scaled_rows[:, None] * mult_full[None, :]
        ratios = sym_counts / denom
        new_rows = mult_rows * jnp.sum(ratios * scaled[None, :], axis=1)
        terms = gamma_rows * jnp.sum(ratios * mult_full[None, :], axis=1)
        term_rows = lax.psum(terms, "win")
        raw_rows = count_rows / term_rows
        if sweep + 1 < ITERS:
            raw_full, mult_full = (
                lax.all_gather(raw_rows, "frames", axis=0, tiled=True),
                lax.all_gather(new_rows, "frames", axis=0, tiled=True),
            )
        else:
            raw_full = lax.all_gather(raw_rows, "frames", axis=0, tiled=True)
        weights = raw_full / jnp.sum(raw_full)
        mult_rows = new_rows
    weight_rows = lax.dynamic_slice_in_dim(weights, first, rows, 0)
    free_energy = -jnp.log(states * weight_rows)
    log_multipliers = jnp.log(mult_rows * states / window_total)[None, :]
    return (free_energy, log_multipliers)


def solution(mesh):
    placed = (P("win", "frames", None), P("win"), P("win", None), P("win", None))
    return jax.shard_map(
        shards,
        mesh=mesh,
        in_specs=placed,
        out_specs=(P("frames"), P("win", "frames")),
        check_vma=False,
    )
```

profile of v0, /device:TPU:0, one launch (start us, length us, event | category | flops | bytes accessed | tf_op | source)
XLA Modules:
  0.0 147.7 jit_solution(16507466639481832255)
XLA Ops:
  7.2 0.0 all-gather.2.cloned.1.call-start
  7.2 1.3 convert_element_type.11
  8.5 1.3 collective-permute-start
  9.8 1.3 convert_bitcast_fusion
  11.1 0.6 collective-permute-done
  11.7 0.9 pad_maximum_fusion
  12.5 0.0 all-gather.2.cloned.1.call-update
  13.2 0.8 broadcast_multiply_fusion
  14.0 0.8 fusion.6
  14.8 25.7 %all-gather.2.cloned.1.call-done = bf16[288,4096]{1,0:T(8,128)(2,1)} async-done(((bf16[72,4096]{1,0:T(8,128)(2,1)}), bf16[288,4096]{1,0:T(8,128)(2,1)}) %all-gather.2.cloned.1.call-update) | async-done | bytes 2359312 | tf_op jit(solution)/shard_map/all_gather | solution.py:55
  40.5 2.9 %fusion.10 = (bf16[4,64,4096]{2,1,0:T(8,128)(2,1)S(1)}, bf16[4,64,4096]{2,1,0:T(8,128)(2,1)S(1)}) fusion(bf16[4,72,4096]{2,1,0:T(8,128)(2,1)} %bitcast.23, s32[]{:T(128)S(6)} %select_n.20), kind=kLoop, calls=%fused_computation.30 | loop fusion | bytes 8388612 | tf_op jit(solution)/shard_map/slice | solution.py:22
  43.4 0.0 copy-start.1
  43.4 0.4 bitcast_select_fusion
  43.8 0.9 copy-done.1
  44.8 8.1 %fusion.1 = f32[1024,4096]{1,0:T(8,128)} fusion(bf16[256,4096]{1,0:T(8,128)(2,1)S(1)} %bitcast_select_fusion, bf16[256,4096]{1,0:T(8,128)(2,1)S(1)} %bitcast.21, s32[]{:T(128)S(6)} %select_n.18), kind=kOutput, calls=%fused_computation.10 | convolution fusion | flops 2147483648 | bytes 19398660 | tf_op jit(solution)/shard_map/tr,ts->rs/dot_general | solution.py:33
  52.9 7.8 %fusion.11 = (f32[1024]{0:T(1024)S(1)}, f32[1024,4096]{1,0:T(8,128)S(1)}) fusion(f32[1024,4096]{1,0:T(8,128)} %fusion.1, bf16[256,4096]{1,0:T(8,128)(2,1)} %bitcast.22, bf16[256,4096]{1,0:T(8,128)(2,1)S(1)} %bitcast_select_fusion, s32[]{:T(128)S(6)} %select_n.18), kind=kOutput, calls=%fused_computation.31 | convolution fusion | flops 2155871232 | bytes 36179972 | tf_op jit(solution)/shard_map/tr,ts->rs/dot_general | solution.py:34
  60.7 0.0 copy-start
  60.7 5.2 %all_gather.16 = f32[4096]{0:T(1024)S(1)} all-gather(f32[1024]{0:T(1024)S(1)} %broadcast_multiply_fusion.1), channel_id=1, replica_groups=mesh['frames'=4,'win'=8] {'frames'}, dimensions={0}, use_global_device_ids=true | all-gather | bytes 20480 | tf_op jit(solution)/shard_map/all_gather | solution.py:61
  65.9 0.5 copy-done
  66.4 6.2 %multiply_reduce_fusion.2 = (f32[1024]{0:T(1024)S(1)}, f32[1024]{0:T(1024)S(1)}) fusion(f32[4096]{0:T(1024)S(1)} %all_gather.16, f32[4096]{0:T(1024)S(1)} %bitcast.26, f32[1024,4096]{1,0:T(8,128)S(1)} %get-tuple-element.13, f32[1024]{0:T(1024)S(1)} %dynamic-slice_multiply_fusion, f32[1024]{0:T(1024)S(1)} %broadcast_multiply_fusion.1), kind=kLoop, calls=%fused_computation.3 | loop fusion | flops 33552384 | bytes 16826368 | tf_op jit(solution)/shard_map/reduce_sum | solution.py:71
  72.6 5.2 %all_gather.18 = f32[4096]{0:T(1024)S(1)} all-gather(f32[1024]{0:T(1024)S(1)} %fusion.9), channel_id=1, replica_groups=mesh['frames'=4,'win'=8] {'frames'}, dimensions={0}, use_global_device_ids=true | all-gather | bytes 20480 | tf_op jit(solution)/shard_map/all_gather | solution.py:77
  77.8 21.6 %all-reduce.1 = (f32[1024]{0:T(1024)S(1)}, f32[1024]{0:T(1024)S(1)}) all-reduce(f32[1024]{0:T(1024)S(1)} %broadcast_multiply_fusion.1, f32[1024]{0:T(1024)S(1)} %mul.185), channel_id=1, replica_groups=mesh['frames'=4,'win'=8] {'win'}, use_global_device_ids=true, to_apply=%region_1.2 | all-reduce | flops 2048 | bytes 16384 | tf_op jit(solution)/shard_map/psum | solution.py:63
  99.4 5.2 %all_gather.17 = f32[4096]{0:T(1024)S(1)} all-gather(f32[1024]{0:T(1024)S(1)} %div.38), channel_id=1, replica_groups=mesh['frames'=4,'win'=8] {'frames'}, dimensions={0}, use_global_device_ids=true | all-gather | bytes 20480 | tf_op jit(solution)/shard_map/all_gather | solution.py:76
  104.6 0.6 reduce_sum.79
  105.2 0.6 reduce_sum.75
  105.8 0.7 divide_multiply_fusion
  106.5 9.0 %multiply_reduce_fusion = (f32[1024]{0:T(1024)S(1)}, f32[1024]{0:T(1024)S(1)}) fusion(f32[4096]{0:T(1024)S(1)} %divide_multiply_fusion, f32[4096]{0:T(1024)S(1)} %all_gather.18, f32[1024,4096]{1,0:T(8,128)} %copy-done, f32[1024]{0:T(1024)S(1)} %dynamic_slice.33, f32[1024]{0:T(1024)S(1)} %fusion.9), kind=kLoop, calls=%fused_computation | loop fusion | flops 33552384 | bytes 16826368 | tf_op jit(solution)/shard_map/reduce_sum | solution.py:70
  115.5 17.1 %psum.23 = f32[1024]{0:T(1024)S(1)} all-reduce(f32[1024]{0:T(1024)S(1)} %mul.193), channel_id=1, replica_groups=mesh['frames'=4,'win'=8] {'win'}, use_global_device_ids=true, to_apply=%region_7.8 | all-reduce | flops 1024 | bytes 8192 | tf_op jit(solution)/shard_map/psum | solution.py:72
  132.7 5.2 %all_gather.19 = f32[4096]{0:T(1024)S(1)} all-gather(f32[1024]{0:T(1024)S(1)} %div.42), channel_id=1, replica_groups=mesh['frames'=4,'win'=8] {'frames'}, dimensions={0}, use_global_device_ids=true | all-gather | bytes 20480 | tf_op jit(solution)/shard_map/all_gather | solution.py:80
  137.9 0.6 reduce_sum.77
  138.5 1.3 fusion.5
  139.7 1.2 divide_log_fusion
  (10 shorter events, 0.1 us)
Async XLA Ops:
  7.2 33.3 %all-gather.2.cloned.1.call-start = ((), (), s32[]{:S(2)}) async-start(), calls=%async_computation | async-start | bytes 2949120 | tf_op jit(solution)/shard_map/all_gather | solution.py:55
  8.5 3.1 %collective-permute-start = (bf16[8,4096]{1,0:T(8,128)(2,1)S(1)}, bf16[8,4096]{1,0:T(8,128)(2,1)S(1)}, u32[]{:S(2)}, u32[]{:S(2)}) collective-permute-start(bf16[8,4096]{1,0:T(8,128)(2,1)S(1)} %slice_bitcast_fusion), channel_id=1, source_target_pairs={{8,0},{16,8},{24,16},{9,1},{17,9},{25,17},{10,2},{18,10},{26,18},{... | collective-permute-start | bytes 196616 | tf_op jit(solution)/shard_map/ppermute | solution.py:14
  43.4 1.4 copy-start.1
  60.7 5.7 %copy-start = (f32[1024,4096]{1,0:T(8,128)}, f32[1024,4096]{1,0:T(8,128)S(1)}, u32[]{:S(2)}) copy-start(f32[1024,4096]{1,0:T(8,128)S(1)} %get-tuple-element.13) | copy-start | bytes 50331652
Sparse Core Ops, SparseCore 0:
  12.7 27.7 all-gather.1
where the time goes:
time: 148 us
  blocking collectives  59.6 us (40%)
  waiting for transfers between devices  26.2 us (18%)
  other arithmetic  25.5 us (17%)
  matrix products  15.9 us (11%)
  between operations  14.8 us (10%)
  local copies, waits for them, and re-layouts  4.38 us (3%)
    all_gather x1, waiting for transfers between devices, shards(): lax.all_gather(extended, 'frames', axis=0, tiled=True)  25.7 us
    psum x1, blocking collectives, shards(): count_rows = lax.psum(mult_rows, 'win')  21.6 us
    psum x1, blocking collectives, shards(): term_rows = lax.psum(terms, 'win')  17.1 us
    reduce_sum x1, other arithmetic, shards(): new_rows = mult_rows * jnp.sum(ratios * scaled[None, :], axis=1)  8.98 us
    dot_general x1, matrix products, add_pair(): jnp.einsum('tr,ts->rs', current_cols, later, preferred_element_type=jnp.f...  8.12 us
    dot_general x1, matrix products, add_pair(): jnp.einsum('tr,ts->rs', later_cols, current, preferred_element_type=jnp.f...  7.76 us
    reduce_sum x1, other arithmetic, shards(): terms = gamma_rows * jnp.sum(ratios * mult_full[None, :], axis=1)  6.19 us
    all_gather x1, blocking collectives, shards(): mult_full = lax.all_gather(mult_rows, 'frames', axis=0, tiled=True)  5.21 us
  transfers between devices with their start and end apart: 2, of which 2 were waited for; matrix products, arithmetic and copies ran while one was open for 2% of the time, Pallas kernels for 0%

commit v1 on v0

--- a/solution.py
+++ b/solution.py
@@ -6,6 +6,17 @@
 LAGMAX = 8
 ITERS = 2
 bias_unit = 1.0 / 128.0
+
+
+def collect(x, axis, dim):
+    ways = lax.axis_size(axis)
+    pieces = [x]
+    for far in range(1, ways):
+        pieces.append(
+            lax.ppermute(pieces[far - 1], axis, [(d, (d - 1) % ways) for d in range(ways)])
+        )
+    line = jnp.concatenate(pieces, axis=dim)
+    return jnp.roll(line, lax.axis_index(axis) * x.shape[dim], axis=dim)
 
 
 def shifted(block, axis, distance):
@@ -51,9 +62,7 @@
     segment_ext = jnp.concatenate([segment_row, jnp.full((LAGMAX,), -1, jnp.int32)])
     valid_all = segment_row == lax.dynamic_slice_in_dim(segment_ext, lag_time, frames_all, 0)
     empty = jnp.zeros((rows, states), jnp.float32)
-    current, later = split_rows(
-        lax.all_gather(extended, "frames", axis=0, tiled=True), frames_dev, lag_time, valid_all
-    )
+    current, later = split_rows(collect(extended, "frames", 0), frames_dev, lag_time, valid_all)
     sym_counts = add_pair(empty, current, later, first, rows)
     gammas = jnp.exp(-bias_codes[0].astype(jnp.float32) * bias_unit)
     gamma_rows = lax.dynamic_slice_in_dim(gammas, first, rows, 0)

time: 148 us -> 142 us (0.959)
  between operations: 14.8 us -> 1.43 us
  starting transfers between devices: 1.33 us -> 8.52 us
  local copies, waits for them, and re-layouts: 4.38 us -> 11.2 us
  waiting for transfers between devices: 26.2 us -> 19.4 us
    all_gather x1 -> x0, waiting for transfers between devices: 25.7 us -> none  [shards(): lax.all_gather(extended, 'frames', axis=0, tiled=True)]
    ppermute x0 -> x3, waiting for transfers between devices: none -> 19.1 us  [collect(): lax.ppermute(pieces[far - 1], axis, [(d, (d - 1) % ways) for d in range(w...]
    ppermute x0 -> x3, starting transfers between devices: none -> 7.24 us  [collect(): lax.ppermute(pieces[far - 1], axis, [(d, (d - 1) % ways) for d in range(w...]
    unnamed x4 -> x12, local copies, waits for them, and re-layouts: 1.43 us -> 7.36 us
    convert_element_type x2 -> x0, other arithmetic: 2.56 us -> none  [shards(): member = memberships[0].astype(jnp.bfloat16)]
    dynamic_slice x0 -> x1, local copies, waits for them, and re-layouts: none -> 2.23 us  [collect(): return jnp.roll(line, lax.axis_index(axis) * x.shape[dim], axis=dim)]
    slice x1, local copies, waits for them, and re-layouts: 2.92 us -> 0.7 us  [split_rows(): current = shaped[:, :frames_dev].reshape(number * frames_dev, states)]
    unnamed x0 -> x1, other arithmetic: none -> 2.12 us
  transfers between devices with their start and end apart: 2 -> 4, of which waited for: 2 -> 4; matrix products, arithmetic and copies ran while one was open for 2% -> 3% of each run, Pallas kernels for 0% -> 0%
where the time goes in v1:
time: 142 us
  blocking collectives  60.9 us (43%)
  other arithmetic  24.2 us (17%)
  waiting for transfers between devices  19.4 us (14%)
  matrix products  15.9 us (11%)
  local copies, waits for them, and re-layouts  11.2 us (8%)
  starting transfers between devices  8.52 us (6%)
  between operations  1.43 us (1%)
    psum x1, blocking collectives, shards(): count_rows = lax.psum(mult_rows, 'win')  21.9 us
    ppermute x3, waiting for transfers between devices, collect(): lax.ppermute(pieces[far - 1], axis, [(d, (d - 1) % ways) for d in range(w...  19.1 us
    psum x1, blocking collectives, shards(): term_rows = lax.psum(terms, 'win')  17.1 us
    reduce_sum x1, other arithmetic, shards(): new_rows = mult_rows * jnp.sum(ratios * scaled[None, :], axis=1)  8.98 us
    dot_general x1, matrix products, add_pair(): jnp.einsum('tr,ts->rs', current_cols, later, preferred_element_type=jnp.f...  8.12 us
    dot_general x1, matrix products, add_pair(): jnp.einsum('tr,ts->rs', later_cols, current, preferred_element_type=jnp.f...  7.77 us
    unnamed x12, local copies, waits for them, and re-layouts  7.36 us
    ppermute x3, starting transfers between devices, collect(): lax.ppermute(pieces[far - 1], axis, [(d, (d - 1) % ways) for d in range(w...  7.24 us
  transfers between devices with their start and end apart: 4, of which 4 were waited for; matrix products, arithmetic and copies ran while one was open for 3% of the time, Pallas kernels for 0%

profile of v1, /device:TPU:0, one launch (start us, length us, event | category | flops | bytes accessed | tf_op | source)
XLA Modules:
  0.0 141.5 jit_solution(13948259230932229967)
XLA Ops:
  0.6 2.1 %constant_dynamic-update-slice_fusion.9 = (bf16[576,4096]{1,0:T(8,128)(2,1)}, bf16[1,64,4096]{2,1,0:T(8,128)(2,1)S(1)}) fusion(f32[1,64,4096]{2,1,0:T(8,128)} %param.4), kind=kLoop, calls=%fused_computation.22 | loop fusion | flops 262143 | bytes 2097152
  2.8 1.3 collective-permute-start
  4.7 0.8 fusion.8
  5.9 3.4 %collective-permute-start.1 = (bf16[72,4096]{1,0:T(8,128)(2,1)S(1)}, bf16[72,4096]{1,0:T(8,128)(2,1)S(1)}, u32[]{:S(2)}, u32[]{:S(2)}) collective-permute-start(bf16[72,4096]{1,0:T(8,128)(2,1)S(1)} %pad_maximum_fusion), channel_id=1, source_target_pairs={{0,24},{8,0},{16,8},{24,16},{1,25},{9,1},{17,9},{25,17},{2,26},{10... | collective-permute-start | bytes 1769480 | tf_op jit(solution)/shard_map/ppermute | solution.py:16
  9.4 0.7 broadcast_multiply_fusion
  10.1 6.7 %collective-permute-done.1 = bf16[72,4096]{1,0:T(8,128)(2,1)S(1)} collective-permute-done((bf16[72,4096]{1,0:T(8,128)(2,1)S(1)}, bf16[72,4096]{1,0:T(8,128)(2,1)S(1)}, u32[]{:S(2)}, u32[]{:S(2)}) %collective-permute-start.1) | collective-permute-done | bytes 589856 | tf_op jit(solution)/shard_map/ppermute | solution.py:16
  16.8 1.9 %collective-permute-start.2 = (bf16[72,4096]{1,0:T(8,128)(2,1)S(1)}, bf16[72,4096]{1,0:T(8,128)(2,1)S(1)}, u32[]{:S(2)}, u32[]{:S(2)}) collective-permute-start(bf16[72,4096]{1,0:T(8,128)(2,1)S(1)} %collective-permute-done.1), channel_id=1, source_target_pairs={{0,24},{8,0},{16,8},{24,16},{1,25},{9,1},{17,9},{25,17},{2,26},{10... | collective-permute-start | bytes 1769480 | tf_op jit(solution)/shard_map/ppermute | solution.py:16
  19.3 6.8 %collective-permute-done.2 = bf16[72,4096]{1,0:T(8,128)(2,1)S(1)} collective-permute-done((bf16[72,4096]{1,0:T(8,128)(2,1)S(1)}, bf16[72,4096]{1,0:T(8,128)(2,1)S(1)}, u32[]{:S(2)}, u32[]{:S(2)}) %collective-permute-start.2) | collective-permute-done | bytes 589856 | tf_op jit(solution)/shard_map/ppermute | solution.py:16
  26.1 1.9 %collective-permute-start.3 = (bf16[72,4096]{1,0:T(8,128)(2,1)S(1)}, bf16[72,4096]{1,0:T(8,128)(2,1)S(1)}, u32[]{:S(2)}, u32[]{:S(2)}) collective-permute-start(bf16[72,4096]{1,0:T(8,128)(2,1)S(1)} %collective-permute-done.2), channel_id=1, source_target_pairs={{0,24},{8,0},{16,8},{24,16},{1,25},{9,1},{17,9},{25,17},{2,26},{10... | collective-permute-start | bytes 1769480 | tf_op jit(solution)/shard_map/ppermute | solution.py:16
  28.0 0.9 constant_dynamic-update-slice_fusion.7
  28.8 0.9 constant_dynamic-update-slice_fusion.6
  29.7 5.7 %collective-permute-done.3 = bf16[72,4096]{1,0:T(8,128)(2,1)S(1)} collective-permute-done((bf16[72,4096]{1,0:T(8,128)(2,1)S(1)}, bf16[72,4096]{1,0:T(8,128)(2,1)S(1)}, u32[]{:S(2)}, u32[]{:S(2)}) %collective-permute-start.3) | collective-permute-done | bytes 589856 | tf_op jit(solution)/shard_map/ppermute | solution.py:16
  35.4 0.9 constant_dynamic-update-slice_fusion.5
  36.3 0.8 constant_dynamic-update-slice_fusion.4
  37.7 0.9 constant_dynamic-update-slice_fusion.2
  38.6 0.9 constant_dynamic-update-slice_fusion.1
  39.4 0.9 constant_dynamic-update-slice_fusion
  40.3 2.2 %constant_dynamic-slice_fusion.2 = bf16[288,4096]{1,0:T(8,128)(2,1)S(1)} fusion(bf16[576,4096]{1,0:T(8,128)(2,1)} %constant_dynamic-update-slice_fusion, s32[]{:T(128)S(6)} %select_n.32), kind=kLoop, calls=%fused_computation.38 | loop fusion | bytes 4718596 | tf_op jit(solution)/shard_map/jit(_roll_dynamic)/dynamic_slice | solution.py:19
  42.5 0.7 fusion.10
  43.6 0.9 copy-done.1
  44.6 8.1 %fusion.1 = f32[1024,4096]{1,0:T(8,128)} fusion(bf16[256,4096]{1,0:T(8,128)(2,1)S(1)} %bitcast_select_fusion, bf16[256,4096]{1,0:T(8,128)(2,1)S(1)} %bitcast.23, s32[]{:T(128)S(6)} %select_n.33), kind=kOutput, calls=%fused_computation.10 | convolution fusion | flops 2147483648 | bytes 19398660 | tf_op jit(solution)/shard_map/tr,ts->rs/dot_general | solution.py:44
  52.7 7.8 %fusion.11 = (f32[1024]{0:T(1024)S(1)}, f32[1024,4096]{1,0:T(8,128)S(1)}) fusion(f32[1024,4096]{1,0:T(8,128)} %fusion.1, bf16[256,4096]{1,0:T(8,128)(2,1)} %bitcast.24, bf16[256,4096]{1,0:T(8,128)(2,1)S(1)} %bitcast_select_fusion, s32[]{:T(128)S(6)} %select_n.33), kind=kOutput, calls=%fused_computation.42 | convolution fusion | flops 2155871232 | bytes 36179972 | tf_op jit(solution)/shard_map/tr,ts->rs/dot_general | solution.py:45
  60.5 6.2 %all_gather.12 = f32[4096]{0:T(1024)S(1)} all-gather(f32[1024]{0:T(1024)S(1)} %broadcast_multiply_fusion.1), channel_id=1, replica_groups=mesh['frames'=4,'win'=8] {'frames'}, dimensions={0}, use_global_device_ids=true | all-gather | bytes 20480 | tf_op jit(solution)/shard_map/all_gather | solution.py:70
  66.8 6.2 %multiply_reduce_fusion.2 = (f32[1024]{0:T(1024)S(1)}, f32[1024]{0:T(1024)S(1)}) fusion(f32[4096]{0:T(1024)S(1)} %all_gather.12, f32[4096]{0:T(1024)S(1)} %bitcast.28, f32[1024,4096]{1,0:T(8,128)S(1)} %get-tuple-element.15, f32[1024]{0:T(1024)S(1)} %dynamic-slice_multiply_fusion, f32[1024]{0:T(1024)S(1)} %broadcast_multiply_fusion.1), kind=kLoop, calls=%fused_computation.3 | loop fusion | flops 33552384 | bytes 16826368 | tf_op jit(solution)/shard_map/reduce_sum | solution.py:80
  73.0 5.2 %all_gather.14 = f32[4096]{0:T(1024)S(1)} all-gather(f32[1024]{0:T(1024)S(1)} %fusion.9), channel_id=1, replica_groups=mesh['frames'=4,'win'=8] {'frames'}, dimensions={0}, use_global_device_ids=true | all-gather | bytes 20480 | tf_op jit(solution)/shard_map/all_gather | solution.py:86
  78.2 21.9 %all-reduce.1 = (f32[1024]{0:T(1024)S(1)}, f32[1024]{0:T(1024)S(1)}) all-reduce(f32[1024]{0:T(1024)S(1)} %broadcast_multiply_fusion.1, f32[1024]{0:T(1024)S(1)} %mul.189), channel_id=1, replica_groups=mesh['frames'=4,'win'=8] {'win'}, use_global_device_ids=true, to_apply=%region_1.2 | all-reduce | flops 2048 | bytes 16384 | tf_op jit(solution)/shard_map/psum | solution.py:72
  100.1 5.2 %all_gather.13 = f32[4096]{0:T(1024)S(1)} all-gather(f32[1024]{0:T(1024)S(1)} %div.38), channel_id=1, replica_groups=mesh['frames'=4,'win'=8] {'frames'}, dimensions={0}, use_global_device_ids=true | all-gather | bytes 20480 | tf_op jit(solution)/shard_map/all_gather | solution.py:85
  107.2 9.0 %multiply_reduce_fusion = (f32[1024]{0:T(1024)S(1)}, f32[1024]{0:T(1024)S(1)}) fusion(f32[4096]{0:T(1024)S(1)} %divide_multiply_fusion, f32[4096]{0:T(1024)S(1)} %all_gather.14, f32[1024,4096]{1,0:T(8,128)} %copy-done, f32[1024]{0:T(1024)S(1)} %dynamic_slice.38, f32[1024]{0:T(1024)S(1)} %fusion.9), kind=kLoop, calls=%fused_computation | loop fusion | flops 33552384 | bytes 16826368 | tf_op jit(solution)/shard_map/reduce_sum | solution.py:79
  116.2 17.1 %psum.23 = f32[1024]{0:T(1024)S(1)} all-reduce(f32[1024]{0:T(1024)S(1)} %mul.197), channel_id=1, replica_groups=mesh['frames'=4,'win'=8] {'win'}, use_global_device_ids=true, to_apply=%region_7.8 | all-reduce | flops 1024 | bytes 8192 | tf_op jit(solution)/shard_map/psum | solution.py:81
  133.3 5.2 %all_gather.15 = f32[4096]{0:T(1024)S(1)} all-gather(f32[1024]{0:T(1024)S(1)} %div.42), channel_id=1, replica_groups=mesh['frames'=4,'win'=8] {'frames'}, dimensions={0}, use_global_device_ids=true | all-gather | bytes 20480 | tf_op jit(solution)/shard_map/all_gather | solution.py:89
  139.1 1.3 fusion.5
  140.4 1.2 divide_log_fusion
  (22 shorter events, 4.5 us)
Async XLA Ops:
  2.8 3.1 %collective-permute-start = (bf16[8,4096]{1,0:T(8,128)(2,1)S(1)}, bf16[8,4096]{1,0:T(8,128)(2,1)S(1)}, u32[]{:S(2)}, u32[]{:S(2)}) collective-permute-start(bf16[8,4096]{1,0:T(8,128)(2,1)S(1)} %slice_bitcast_fusion), channel_id=1, source_target_pairs={{8,0},{16,8},{24,16},{9,1},{17,9},{25,17},{10,2},{18,10},{26,18},{... | collective-permute-start | bytes 196616 | tf_op jit(solution)/shard_map/ppermute | solution.py:25
  5.9 10.8 %collective-permute-start.1 = (bf16[72,4096]{1,0:T(8,128)(2,1)S(1)}, bf16[72,4096]{1,0:T(8,128)(2,1)S(1)}, u32[]{:S(2)}, u32[]{:S(2)}) collective-permute-start(bf16[72,4096]{1,0:T(8,128)(2,1)S(1)} %pad_maximum_fusion), channel_id=1, source_target_pairs={{0,24},{8,0},{16,8},{24,16},{1,25},{9,1},{17,9},{25,17},{2,26},{10... | collective-permute-start | bytes 1769480 | tf_op jit(solution)/shard_map/ppermute | solution.py:16
  16.8 9.3 %collective-permute-start.2 = (bf16[72,4096]{1,0:T(8,128)(2,1)S(1)}, bf16[72,4096]{1,0:T(8,128)(2,1)S(1)}, u32[]{:S(2)}, u32[]{:S(2)}) collective-permute-start(bf16[72,4096]{1,0:T(8,128)(2,1)S(1)} %collective-permute-done.1), channel_id=1, source_target_pairs={{0,24},{8,0},{16,8},{24,16},{1,25},{9,1},{17,9},{25,17},{2,26},{10... | collective-permute-start | bytes 1769480 | tf_op jit(solution)/shard_map/ppermute | solution.py:16
  26.1 9.3 %collective-permute-start.3 = (bf16[72,4096]{1,0:T(8,128)(2,1)S(1)}, bf16[72,4096]{1,0:T(8,128)(2,1)S(1)}, u32[]{:S(2)}, u32[]{:S(2)}) collective-permute-start(bf16[72,4096]{1,0:T(8,128)(2,1)S(1)} %collective-permute-done.2), channel_id=1, source_target_pairs={{0,24},{8,0},{16,8},{24,16},{1,25},{9,1},{17,9},{25,17},{2,26},{10... | collective-permute-start | bytes 1769480 | tf_op jit(solution)/shard_map/ppermute | solution.py:16
  43.2 1.4 copy-start.1
  60.5 12.5 %copy-start = (f32[1024,4096]{1,0:T(8,128)}, f32[1024,4096]{1,0:T(8,128)S(1)}, u32[]{:S(2)}) copy-start(f32[1024,4096]{1,0:T(8,128)S(1)} %get-tuple-element.15) | copy-start | bytes 50331652
